TPU v7x, 32 devices: a whole 2x2x4 slice. The times are simulated.
32 devices in a mesh: groups: 2 (over x), dp: 16 (over z, y, core).
Axes of the slice: x: 2, y: 2, z: 4, core: 2. Of those that a mesh axis runs over, the one named last changes fastest.
Arguments:
- tokens: bfloat16 [12288, 8192], P(('groups', 'dp')), parts along dimension 0, may hold values from -6 to 6
- base_weight: bfloat16 [8192, 768], P('dp'), may hold values from -0.0625 to 0.0625
- down_stack: bfloat16 [8192, 512], P('dp'), may hold values from -0.0625 to 0.0625
- up_stack: bfloat16 [512, 768], replicated, may hold values from -0.75 to 0.75
- adapter_scale: float32 [8], replicated, may hold values from 0.5 to 2
- lengths: int32 [64], P(('groups', 'dp')), parts along dimension 0, may hold values from 1 to 256, as said below
- adapter_ids: int32 [64], P(('groups', 'dp')), parts along dimension 0, may hold values from 0 to 7
Outputs:
- projected: bfloat16 [12288, 768], P(('groups', 'dp')), parts along dimension 0
There are 2 independent parts, one for each index of `groups`. A program takes and returns all parts, laid end to end along the dimension named above; an argument that names none is the same for every part. Nothing has to cross between parts.
Inputs may be any that keep to these rules, and one draw needn't show every extreme that they name: `lengths`: each index of dp holds two requests whose block counts ceil(length / 128) add up to exactly 3.
All inputs are finite; a program needn't handle non-finite values.
Results may differ from a plain program's by a relative error of at most 0.0042.
Values may be sent and summed in bfloat16 or wider, within the bound.
A program may use at most 128 MiB of HBM per device.

v0:
```python
import jax
import jax.numpy as jnp
from jax import lax
from jax.sharding import PartitionSpec as P

RANK = 64
BLOCK = 128


def layout(lengths, adapter_ids, row_count):
    counts = (lengths + BLOCK - 1) // BLOCK
    position = jnp.arange(row_count, dtype=jnp.int32)
    boundary = counts[0] * BLOCK
    second = position >= boundary
    offset = jnp.where(second, position - boundary, position)
    is_live = offset < jnp.where(second, lengths[1], lengths[0])
    token_adapter = jnp.where(second, adapter_ids[1], adapter_ids[0])
    return (is_live, token_adapter)


def local(tokens, base_weight, down_stack, up_stack, adapter_scale, lengths, adapter_ids):
    row_count = tokens.shape[0]
    num_blocks = row_count // BLOCK
    adapters = down_stack.shape[1] // RANK
    is_live, token_adapter = layout(lengths, adapter_ids, row_count)
    adapter_per_block = token_adapter.reshape(num_blocks, BLOCK)[:, 0]
    w_piece = lax.all_gather(base_weight, "dp", axis=0, tiled=True)
    a_piece = lax.all_gather(down_stack, "dp", axis=0, tiled=True)
    width_dev = w_piece.shape[0]
    base_projection_share = jnp.dot(tokens, w_piece, preferred_element_type=jnp.float32)
    down_split = a_piece.reshape(width_dev, adapters, RANK)
    selected_adapter = jnp.take(down_split, adapter_per_block, axis=1)
    token_block_groups = tokens.reshape(num_blocks, BLOCK, width_dev)
    low_part = jnp.einsum(
        "wmu,uwi->wmi", token_block_groups, selected_adapter, preferred_element_type=jnp.float32
    )
    low_rank = low_part.reshape(row_count, RANK)
    low_rank = low_rank.astype(jnp.bfloat16)
    onehot = token_adapter[:, None] == jnp.arange(adapters, dtype=jnp.int32)[None, :]
    widened = jnp.where(
        onehot[:, :, None], low_rank[:, None, :], jnp.zeros((), jnp.bfloat16)
    ).reshape(row_count, adapters * RANK)
    adapter_out = jnp.dot(widened, up_stack, preferred_element_type=jnp.float32)
    token_scale = jnp.sum(jnp.where(onehot, adapter_scale[None, :], 0.0), axis=1)
    result = jnp.where(
        is_live[:, None], base_projection_share + token_scale[:, None] * adapter_out, 0.0
    )
    return result.astype(jnp.bfloat16)


def solution(mesh):
    in_specs = (
        P(("groups", "dp"), None),
        P("dp", None),
        P("dp", None),
        P(),
        P(),
        P(("groups", "dp")),
        P(("groups", "dp")),
    )
    out_specs = P(("groups", "dp"), None)
    return jax.shard_map(local, mesh=mesh, in_specs=in_specs, out_specs=out_specs, check_vma=False)
```

profile of v0, /device:TPU:0, one launch (start us, length us, event | category | flops | bytes accessed | tf_op | source)
XLA Modules:
  0.0 209.0 jit_solution(384807473434805781)
XLA Ops:
  6.5 0.0 copy-start
  6.5 0.0 all-gather.5.cloned.1.call-start
  6.5 2.1 %copy.8 = bf16[512,512]{0,1:T(8,128)(2,1)} copy(bf16[512,512]{1,0:T(8,128)(2,1)} %param.9) | data formatting | bytes 1048576 | tf_op args[2]
  8.7 0.0 all-gather.5.cloned.1.call-update
  8.7 0.0 all-gather.3.cloned.1.call-start
  8.7 0.7 all-gather.3.cloned.1.call-update
  9.4 0.7 and_select_fusion
  10.1 1.3 fusion.18
  11.5 1.2 and_bitcast_fusion
  12.7 1.2 fusion.16
  14.0 1.4 fusion.17
  15.3 1.2 select_compare_fusion
  16.6 1.2 fusion.14
  17.8 0.7 select_reduce_fusion
  18.6 71.4 %all-gather.5.cloned.1.call-done = bf16[8192,512]{0,1:T(8,128)(2,1)} async-done(((bf16[512,512]{0,1:T(8,128)(2,1)}), bf16[8192,512]{0,1:T(8,128)(2,1)}) %all-gather.5.cloned.1.call-update) | async-done | bytes 8388624 | tf_op jit(solution)/shard_map/all_gather | solution.py:28
  90.0 5.9 %gather_fusion = bf16[3,8192,64]{1,2,0:T(8,128)(2,1)} fusion(bf16[8192,8,64]{0,2,1:T(8,128)(2,1)} %bitcast.31, s32[1024]{0:T(1024)S(1)} %pad_clamp_fusion), kind=kCustom, calls=%fused_computation | custom fusion | bytes 6291468 | tf_op jit(solution)/shard_map/jit(_take)/gather | solution.py:32
  95.9 6.7 %fusion.11 = bf16[3,8,8,128]{3,2,1,0:T(8,128)(2,1)S(1)} fusion(bf16[3,128,8192]{2,1,0:T(8,128)(2,1)} %bitcast.34, bf16[3,8192,64]{1,2,0:T(8,128)(2,1)} %gather_fusion, pred[3]{0:T(512)(128)(4,1)S(1)} %and_bitcast_fusion), kind=kOutput, calls=%fused_computation.11 | convolution fusion | flops 404250624 | bytes 9486339 | tf_op jit(solution)/shard_map/wmu,uwi->wmi/dot_general | solution.py:34
  102.5 0.1 broadcast_select_fusion
  102.6 88.3 %all-gather.3.cloned.1.call-done = bf16[8192,768]{1,0:T(8,128)(2,1)} async-done(((bf16[512,768]{1,0:T(8,128)(2,1)}), bf16[8192,768]{1,0:T(8,128)(2,1)}) %all-gather.3.cloned.1.call-update) | async-done | bytes 12582928 | tf_op jit(solution)/shard_map/all_gather | solution.py:27
  190.9 9.9 %fusion.19 = f32[384,768]{1,0:T(8,128)S(1)} fusion(bf16[384,8192]{1,0:T(8,128)(2,1)} %param.7, bf16[8192,768]{1,0:T(8,128)(2,1)} %all-gather.3.cloned.1.call-done), kind=kOutput, calls=%fused_computation.33 | convolution fusion | flops 4831838208 | bytes 20054016 | tf_op jit(solution)/shard_map/dot_general | solution.py:30
  200.8 0.0 copy-done
  200.8 1.3 fusion.7
  (3 shorter events, 0.0 us)
Async XLA Ops:
  6.5 194.3 %copy-start = (bf16[512,768]{1,0:T(8,128)(2,1)S(1)}, bf16[512,768]{1,0:T(8,128)(2,1)}, u32[]{:S(2)}) copy-start(bf16[512,768]{1,0:T(8,128)(2,1)} %param.10) | copy-start | bytes 2359300
  6.5 83.4 %all-gather.5.cloned.1.call-start = ((), (), s32[]{:S(2)}) async-start(), calls=%async_computation.1 | async-start | bytes 8912896 | tf_op jit(solution)/shard_map/all_gather | solution.py:28
  8.7 182.2 %all-gather.3.cloned.1.call-start = ((), (), s32[]{:S(2)}) async-start(), calls=%async_computation | async-start | bytes 13369344 | tf_op jit(solution)/shard_map/all_gather | solution.py:27
Sparse Core Ops, SparseCore 0:
  9.5 80.4 all-gather.4
  92.2 98.5 all-gather.2
where the time goes:
time: 209 us
  waiting for transfers between devices  160 us (77%)
  matrix products  17.9 us (9%)
  between operations  13.5 us (6%)
  local copies, waits for them, and re-layouts  10.8 us (5%)
  other arithmetic  6.4 us (3%)
    all_gather x1, waiting for transfers between devices, local(): w_piece = lax.all_gather(base_weight, 'dp', axis=0, tiled=True)  88.3 us
    all_gather x1, waiting for transfers between devices, local(): a_piece = lax.all_gather(down_stack, 'dp', axis=0, tiled=True)  71.4 us
    dot_general x1, matrix products, local(): jnp.dot(tokens, w_piece, preferred_element_type=jnp.float32)  9.92 us
    dot_general x1, matrix products, local(): jnp.einsum('wmu,uwi->wmi', token_block_groups, selected_adapter, preferre...  6.65 us
    gather x1, local copies, waits for them, and re-layouts, local(): selected_adapter = jnp.take(down_split, adapter_per_block, axis=1)  5.9 us
  transfers between devices with their start and end apart: 2, of which 2 were waited for; matrix products, arithmetic and copies ran while one was open for 10% of the time, Pallas kernels for 0%

commit v1 on v0

--- a/solution.py
+++ b/solution.py
@@ -25,7 +25,12 @@
     is_live, token_adapter = layout(lengths, adapter_ids, row_count)
     adapter_per_block = token_adapter.reshape(num_blocks, BLOCK)[:, 0]
     w_piece = lax.all_gather(base_weight, "dp", axis=0, tiled=True)
-    a_piece = lax.all_gather(down_stack, "dp", axis=0, tiled=True)
+    ring = [down_stack]
+    for hop in range(15):
+        ring.append(lax.ppermute(ring[-1], "dp", [(dev, (dev + 1) % 16) for dev in range(16)]))
+    a_piece = jnp.roll(
+        jnp.concatenate(ring[::-1], axis=0), (lax.axis_index("dp") + 1) * ring[0].shape[0], axis=0
+    )
     width_dev = w_piece.shape[0]
     base_projection_share = jnp.dot(tokens, w_piece, preferred_element_type=jnp.float32)
     down_split = a_piece.reshape(width_dev, adapters, RANK)

time: 209 us -> 316 us (1.51)
  waiting for transfers between devices: 160 us -> 215 us
  local copies, waits for them, and re-layouts: 10.8 us -> 61.9 us
    ppermute x0 -> x15, waiting for transfers between devices: none -> 214 us  [local(): lax.ppermute(ring[-1], 'dp', [(dev, (dev + 1) % 16) for dev in range(16)])]
    all_gather x1, waiting for transfers between devices: 88.3 us -> 0.02 us  [local(): w_piece = lax.all_gather(base_weight, 'dp', axis=0, tiled=True)]
    all_gather x1 -> x0, waiting for transfers between devices: 71.4 us -> none  [local(): a_piece = lax.all_gather(down_stack, 'dp', axis=0, tiled=True)]
    unnamed x3 -> x62, local copies, waits for them, and re-layouts: 2.12 us -> 44.7 us
    dynamic_slice x0 -> x1, local copies, waits for them, and re-layouts: none -> 7.72 us  [local(): jnp.roll(jnp.concatenate(ring[::-1], axis=0), (lax.axis_index('dp') + 1)...]
  transfers between devices with their start and end apart: 2 -> 16, of which waited for: 2 -> 15; matrix products, arithmetic and copies ran while one was open for 10% -> 22% of each run, Pallas kernels for 0% -> 0%
where the time goes in v1:
time: 316 us; the launch traced here: 315 us
  waiting for transfers between devices  215 us (68%)
  local copies, waits for them, and re-layouts  61.9 us (20%)
  matrix products  17.4 us (6%)
  between operations  13.6 us (4%)
  other arithmetic  6.62 us (2%)
    ppermute x15, waiting for transfers between devices, local(): lax.ppermute(ring[-1], 'dp', [(dev, (dev + 1) % 16) for dev in range(16)])  214 us
    unnamed x62, local copies, waits for them, and re-layouts  44.7 us
    dot_general x1, matrix products, local(): jnp.dot(tokens, w_piece, preferred_element_type=jnp.float32)  10 us
    dynamic_slice x1, local copies, waits for them, and re-layouts, local(): jnp.roll(jnp.concatenate(ring[::-1], axis=0), (lax.axis_index('dp') + 1)...  7.72 us
  transfers between devices with their start and end apart: 16, of which 15 were waited for; matrix products, arithmetic and copies ran while one was open for 22% of the time, Pallas kernels for 0%

profile of v1, /device:TPU:0, one launch (start us, length us, event | category | flops | bytes accessed | tf_op | source)
XLA Modules:
  0.0 314.7 jit_solution(3125366369604428840)
XLA Ops:
  9.1 11.8 %collective-permute-done = bf16[512,512]{0,1:T(8,128)(2,1)S(1)} collective-permute-done((bf16[512,512]{0,1:T(8,128)(2,1)S(1)}, bf16[512,512]{0,1:T(8,128)(2,1)S(1)}, u32[]{:S(2)}, u32[]{:S(2)}) %collective-permute-start) | collective-permute-done | bytes 524320 | tf_op jit(solution)/shard_map/ppermute | solution.py:30
  20.9 22.4 %collective-permute-done.1 = bf16[512,512]{0,1:T(8,128)(2,1)S(1)} collective-permute-done((bf16[512,512]{0,1:T(8,128)(2,1)S(1)}, bf16[512,512]{0,1:T(8,128)(2,1)S(1)}, u32[]{:S(2)}, u32[]{:S(2)}) %collective-permute-start.1) | collective-permute-done | bytes 524320 | tf_op jit(solution)/shard_map/ppermute | solution.py:30
  43.3 19.7 %collective-permute-done.2 = bf16[512,512]{0,1:T(8,128)(2,1)S(1)} collective-permute-done((bf16[512,512]{0,1:T(8,128)(2,1)S(1)}, bf16[512,512]{0,1:T(8,128)(2,1)S(1)}, u32[]{:S(2)}, u32[]{:S(2)}) %collective-permute-start.2) | collective-permute-done | bytes 524320 | tf_op jit(solution)/shard_map/ppermute | solution.py:30
  63.0 21.6 %collective-permute-done.3 = bf16[512,512]{0,1:T(8,128)(2,1)S(1)} collective-permute-done((bf16[512,512]{0,1:T(8,128)(2,1)S(1)}, bf16[512,512]{0,1:T(8,128)(2,1)S(1)}, u32[]{:S(2)}, u32[]{:S(2)}) %collective-permute-start.3) | collective-permute-done | bytes 524320 | tf_op jit(solution)/shard_map/ppermute | solution.py:30
  84.7 22.7 %collective-permute-done.4 = bf16[512,512]{0,1:T(8,128)(2,1)S(1)} collective-permute-done((bf16[512,512]{0,1:T(8,128)(2,1)S(1)}, bf16[512,512]{0,1:T(8,128)(2,1)S(1)}, u32[]{:S(2)}, u32[]{:S(2)}) %collective-permute-start.4) | collective-permute-done | bytes 524320 | tf_op jit(solution)/shard_map/ppermute | solution.py:30
  108.2 22.7 %collective-permute-done.5 = bf16[512,512]{0,1:T(8,128)(2,1)S(1)} collective-permute-done((bf16[512,512]{0,1:T(8,128)(2,1)S(1)}, bf16[512,512]{0,1:T(8,128)(2,1)S(1)}, u32[]{:S(2)}, u32[]{:S(2)}) %collective-permute-start.5) | collective-permute-done | bytes 524320 | tf_op jit(solution)/shard_map/ppermute | solution.py:30
  131.6 11.3 %collective-permute-done.6 = bf16[512,512]{0,1:T(8,128)(2,1)S(1)} collective-permute-done((bf16[512,512]{0,1:T(8,128)(2,1)S(1)}, bf16[512,512]{0,1:T(8,128)(2,1)S(1)}, u32[]{:S(2)}, u32[]{:S(2)}) %collective-permute-start.6) | collective-permute-done | bytes 524320 | tf_op jit(solution)/shard_map/ppermute | solution.py:30
  143.7 11.3 %collective-permute-done.7 = bf16[512,512]{0,1:T(8,128)(2,1)S(1)} collective-permute-done((bf16[512,512]{0,1:T(8,128)(2,1)S(1)}, bf16[512,512]{0,1:T(8,128)(2,1)S(1)}, u32[]{:S(2)}, u32[]{:S(2)}) %collective-permute-start.7) | collective-permute-done | bytes 524320 | tf_op jit(solution)/shard_map/ppermute | solution.py:30
  155.9 11.3 %collective-permute-done.8 = bf16[512,512]{0,1:T(8,128)(2,1)S(1)} collective-permute-done((bf16[512,512]{0,1:T(8,128)(2,1)S(1)}, bf16[512,512]{0,1:T(8,128)(2,1)S(1)}, u32[]{:S(2)}, u32[]{:S(2)}) %collective-permute-start.8) | collective-permute-done | bytes 524320 | tf_op jit(solution)/shard_map/ppermute | solution.py:30
  168.0 11.3 %collective-permute-done.9 = bf16[512,512]{0,1:T(8,128)(2,1)S(1)} collective-permute-done((bf16[512,512]{0,1:T(8,128)(2,1)S(1)}, bf16[512,512]{0,1:T(8,128)(2,1)S(1)}, u32[]{:S(2)}, u32[]{:S(2)}) %collective-permute-start.9) | collective-permute-done | bytes 524320 | tf_op jit(solution)/shard_map/ppermute | solution.py:30
  180.1 11.3 %collective-permute-done.10 = bf16[512,512]{0,1:T(8,128)(2,1)S(1)} collective-permute-done((bf16[512,512]{0,1:T(8,128)(2,1)S(1)}, bf16[512,512]{0,1:T(8,128)(2,1)S(1)}, u32[]{:S(2)}, u32[]{:S(2)}) %collective-permute-start.10) | collective-permute-done | bytes 524320 | tf_op jit(solution)/shard_map/ppermute | solution.py:30
  192.2 11.4 %collective-permute-done.11 = bf16[512,512]{0,1:T(8,128)(2,1)} collective-permute-done((bf16[512,512]{0,1:T(8,128)(2,1)S(1)}, bf16[512,512]{0,1:T(8,128)(2,1)}, u32[]{:S(2)}, u32[]{:S(2)}) %collective-permute-start.11) | collective-permute-done | bytes 524320 | tf_op jit(solution)/shard_map/ppermute | solution.py:30
  204.5 10.7 %collective-permute-done.12 = bf16[512,512]{0,1:T(8,128)(2,1)} collective-permute-done((bf16[512,512]{0,1:T(8,128)(2,1)}, bf16[512,512]{0,1:T(8,128)(2,1)}, u32[]{:S(2)}, u32[]{:S(2)}) %collective-permute-start.12) | collective-permute-done | bytes 524320 | tf_op jit(solution)/shard_map/ppermute | solution.py:30
  221.8 5.0 %collective-permute-done.13 = bf16[512,512]{0,1:T(8,128)(2,1)S(1)} collective-permute-done((bf16[512,512]{0,1:T(8,128)(2,1)}, bf16[512,512]{0,1:T(8,128)(2,1)S(1)}, u32[]{:S(2)}, u32[]{:S(2)}) %collective-permute-start.13) | collective-permute-done | bytes 524320 | tf_op jit(solution)/shard_map/ppermute | solution.py:30
  228.8 9.3 %collective-permute-done.14 = bf16[512,512]{0,1:T(8,128)(2,1)S(1)} collective-permute-done((bf16[512,512]{0,1:T(8,128)(2,1)S(1)}, bf16[512,512]{0,1:T(8,128)(2,1)S(1)}, u32[]{:S(2)}, u32[]{:S(2)}) %collective-permute-start.14) | collective-permute-done | bytes 524320 | tf_op jit(solution)/shard_map/ppermute | solution.py:30
  241.6 1.9 constant_dynamic-update-slice_fusion.28
  243.5 1.9 constant_dynamic-update-slice_fusion.27
  245.4 1.9 constant_dynamic-update-slice_fusion.26
  254.9 1.9 constant_dynamic-update-slice_fusion.21
  262.7 1.9 constant_dynamic-update-slice_fusion.13
  276.7 7.7 %constant_dynamic-slice_fusion = bf16[8192,512]{0,1:T(8,128)(2,1)} fusion(bf16[16384,512]{0,1:T(8,128)(2,1)} %constant_dynamic-update-slice_fusion, s32[]{:T(128)S(6)} %select_n.79), kind=kLoop, calls=%fused_computation.61 | loop fusion | bytes 16777220 | tf_op jit(solution)/shard_map/jit(_roll_dynamic)/dynamic_slice | solution.py:31
  284.4 5.9 %gather_fusion = bf16[3,8192,64]{1,2,0:T(8,128)(2,1)} fusion(bf16[8192,8,64]{0,2,1:T(8,128)(2,1)} %bitcast.31, s32[1024]{0:T(1024)S(1)} %pad_clamp_fusion), kind=kCustom, calls=%fused_computation | custom fusion | bytes 6291468 | tf_op jit(solution)/shard_map/jit(_take)/gather | solution.py:37
  290.3 6.1 %fusion.11 = bf16[3,8,8,128]{3,2,1,0:T(8,128)(2,1)S(1)} fusion(bf16[3,128,8192]{2,1,0:T(8,128)(2,1)} %bitcast.34, bf16[3,8192,64]{1,2,0:T(8,128)(2,1)} %gather_fusion, pred[3]{0:T(512)(128)(4,1)S(1)} %and_bitcast_fusion), kind=kOutput, calls=%fused_computation.11 | convolution fusion | flops 404250624 | bytes 9486339 | tf_op jit(solution)/shard_map/wmu,uwi->wmi/dot_general | solution.py:39
  296.5 10.0 %fusion.19 = f32[384,768]{1,0:T(8,128)S(1)} fusion(bf16[384,8192]{1,0:T(8,128)(2,1)} %param.7, bf16[8192,768]{1,0:T(8,128)(2,1)} %all-gather.2.cloned.1.call-done), kind=kOutput, calls=%fused_computation.66 | convolution fusion | flops 4831838208 | bytes 20054016 | tf_op jit(solution)/shard_map/dot_general | solution.py:35
  (89 shorter events, 48.1 us)
Async XLA Ops:
  6.5 299.9 %copy-start = (bf16[512,768]{1,0:T(8,128)(2,1)S(1)}, bf16[512,768]{1,0:T(8,128)(2,1)}, u32[]{:S(2)}) copy-start(bf16[512,768]{1,0:T(8,128)(2,1)} %param.10) | copy-start | bytes 2359300
  6.5 289.9 %all-gather.2.cloned.1.call-start = ((), (), s32[]{:S(2)}) async-start(), calls=%async_computation | async-start | bytes 13369344 | tf_op jit(solution)/shard_map/all_gather | solution.py:27
  8.5 12.4 %collective-permute-start = (bf16[512,512]{0,1:T(8,128)(2,1)S(1)}, bf16[512,512]{0,1:T(8,128)(2,1)S(1)}, u32[]{:S(2)}, u32[]{:S(2)}) collective-permute-start(bf16[512,512]{0,1:T(8,128)(2,1)S(1)} %copy.8), channel_id=1, source_target_pairs={{0,1},{1,2},{2,3},{3,4},{4,5},{5,6},{6,7},{7,8},{8,9},{9,10},{10,1... | collective-permute-start | bytes 1572872 | tf_op jit(solution)/shard_map/ppermute | solution.py:30
  20.9 22.4 %collective-permute-start.1 = (bf16[512,512]{0,1:T(8,128)(2,1)S(1)}, bf16[512,512]{0,1:T(8,128)(2,1)S(1)}, u32[]{:S(2)}, u32[]{:S(2)}) collective-permute-start(bf16[512,512]{0,1:T(8,128)(2,1)S(1)} %collective-permute-done), channel_id=1, source_target_pairs={{0,1},{1,2},{2,3},{3,4},{4,5},{5,6},{6,7},{7,8},{8,9},{9,10},{10,1... | collective-permute-start | bytes 1572872 | tf_op jit(solution)/shard_map/ppermute | solution.py:30
  43.3 19.7 %collective-permute-start.2 = (bf16[512,512]{0,1:T(8,128)(2,1)S(1)}, bf16[512,512]{0,1:T(8,128)(2,1)S(1)}, u32[]{:S(2)}, u32[]{:S(2)}) collective-permute-start(bf16[512,512]{0,1:T(8,128)(2,1)S(1)} %collective-permute-done.1), channel_id=1, source_target_pairs={{0,1},{1,2},{2,3},{3,4},{4,5},{5,6},{6,7},{7,8},{8,9},{9,10},{10,1... | collective-permute-start | bytes 1572872 | tf_op jit(solution)/shard_map/ppermute | solution.py:30
  63.0 21.6 %collective-permute-start.3 = (bf16[512,512]{0,1:T(8,128)(2,1)S(1)}, bf16[512,512]{0,1:T(8,128)(2,1)S(1)}, u32[]{:S(2)}, u32[]{:S(2)}) collective-permute-start(bf16[512,512]{0,1:T(8,128)(2,1)S(1)} %collective-permute-done.2), channel_id=1, source_target_pairs={{0,1},{1,2},{2,3},{3,4},{4,5},{5,6},{6,7},{7,8},{8,9},{9,10},{10,1... | collective-permute-start | bytes 1572872 | tf_op jit(solution)/shard_map/ppermute | solution.py:30
  84.7 22.7 %collective-permute-start.4 = (bf16[512,512]{0,1:T(8,128)(2,1)S(1)}, bf16[512,512]{0,1:T(8,128)(2,1)S(1)}, u32[]{:S(2)}, u32[]{:S(2)}) collective-permute-start(bf16[512,512]{0,1:T(8,128)(2,1)S(1)} %collective-permute-done.3), channel_id=1, source_target_pairs={{0,1},{1,2},{2,3},{3,4},{4,5},{5,6},{6,7},{7,8},{8,9},{9,10},{10,1... | collective-permute-start | bytes 1572872 | tf_op jit(solution)/shard_map/ppermute | solution.py:30
  108.2 22.7 %collective-permute-start.5 = (bf16[512,512]{0,1:T(8,128)(2,1)S(1)}, bf16[512,512]{0,1:T(8,128)(2,1)S(1)}, u32[]{:S(2)}, u32[]{:S(2)}) collective-permute-start(bf16[512,512]{0,1:T(8,128)(2,1)S(1)} %collective-permute-done.4), channel_id=1, source_target_pairs={{0,1},{1,2},{2,3},{3,4},{4,5},{5,6},{6,7},{7,8},{8,9},{9,10},{10,1... | collective-permute-start | bytes 1572872 | tf_op jit(solution)/shard_map/ppermute | solution.py:30
  131.6 11.3 %collective-permute-start.6 = (bf16[512,512]{0,1:T(8,128)(2,1)S(1)}, bf16[512,512]{0,1:T(8,128)(2,1)S(1)}, u32[]{:S(2)}, u32[]{:S(2)}) collective-permute-start(bf16[512,512]{0,1:T(8,128)(2,1)S(1)} %collective-permute-done.5), channel_id=1, source_target_pairs={{0,1},{1,2},{2,3},{3,4},{4,5},{5,6},{6,7},{7,8},{8,9},{9,10},{10,1... | collective-permute-start | bytes 1572872 | tf_op jit(solution)/shard_map/ppermute | solution.py:30
  143.7 11.3 %collective-permute-start.7 = (bf16[512,512]{0,1:T(8,128)(2,1)S(1)}, bf16[512,512]{0,1:T(8,128)(2,1)S(1)}, u32[]{:S(2)}, u32[]{:S(2)}) collective-permute-start(bf16[512,512]{0,1:T(8,128)(2,1)S(1)} %collective-permute-done.6), channel_id=1, source_target_pairs={{0,1},{1,2},{2,3},{3,4},{4,5},{5,6},{6,7},{7,8},{8,9},{9,10},{10,1... | collective-permute-start | bytes 1572872 | tf_op jit(solution)/shard_map/ppermute | solution.py:30
  155.9 11.3 %collective-permute-start.8 = (bf16[512,512]{0,1:T(8,128)(2,1)S(1)}, bf16[512,512]{0,1:T(8,128)(2,1)S(1)}, u32[]{:S(2)}, u32[]{:S(2)}) collective-permute-start(bf16[512,512]{0,1:T(8,128)(2,1)S(1)} %collective-permute-done.7), channel_id=1, source_target_pairs={{0,1},{1,2},{2,3},{3,4},{4,5},{5,6},{6,7},{7,8},{8,9},{9,10},{10,1... | collective-permute-start | bytes 1572872 | tf_op jit(solution)/shard_map/ppermute | solution.py:30
  168.0 11.3 %collective-permute-start.9 = (bf16[512,512]{0,1:T(8,128)(2,1)S(1)}, bf16[512,512]{0,1:T(8,128)(2,1)S(1)}, u32[]{:S(2)}, u32[]{:S(2)}) collective-permute-start(bf16[512,512]{0,1:T(8,128)(2,1)S(1)} %collective-permute-done.8), channel_id=1, source_target_pairs={{0,1},{1,2},{2,3},{3,4},{4,5},{5,6},{6,7},{7,8},{8,9},{9,10},{10,1... | collective-permute-start | bytes 1572872 | tf_op jit(solution)/shard_map/ppermute | solution.py:30
  180.1 11.3 %collective-permute-start.10 = (bf16[512,512]{0,1:T(8,128)(2,1)S(1)}, bf16[512,512]{0,1:T(8,128)(2,1)S(1)}, u32[]{:S(2)}, u32[]{:S(2)}) collective-permute-start(bf16[512,512]{0,1:T(8,128)(2,1)S(1)} %collective-permute-done.9), channel_id=1, source_target_pairs={{0,1},{1,2},{2,3},{3,4},{4,5},{5,6},{6,7},{7,8},{8,9},{9,10},{10,1... | collective-permute-start | bytes 1572872 | tf_op jit(solution)/shard_map/ppermute | solution.py:30
  192.2 11.4 %collective-permute-start.11 = (bf16[512,512]{0,1:T(8,128)(2,1)S(1)}, bf16[512,512]{0,1:T(8,128)(2,1)}, u32[]{:S(2)}, u32[]{:S(2)}) collective-permute-start(bf16[512,512]{0,1:T(8,128)(2,1)S(1)} %collective-permute-done.10), channel_id=1, source_target_pairs={{0,1},{1,2},{2,3},{3,4},{4,5},{5,6},{6,7},{7,8},{8,9},{9,10},{10,1... | collective-permute-start | bytes 1572872 | tf_op jit(solution)/shard_map/ppermute | solution.py:30
  203.6 11.6 %collective-permute-start.12 = (bf16[512,512]{0,1:T(8,128)(2,1)}, bf16[512,512]{0,1:T(8,128)(2,1)}, u32[]{:S(2)}, u32[]{:S(2)}) collective-permute-start(bf16[512,512]{0,1:T(8,128)(2,1)} %collective-permute-done.11), channel_id=1, source_target_pairs={{0,1},{1,2},{2,3},{3,4},{4,5},{5,6},{6,7},{7,8},{8,9},{9,10},{10,1... | collective-permute-start | bytes 1572872 | tf_op jit(solution)/shard_map/ppermute | solution.py:30
  203.6 62.9 %copy-start.14 = (bf16[512,512]{0,1:T(8,128)(2,1)S(1)}, bf16[512,512]{0,1:T(8,128)(2,1)}, u32[]{:S(2)}) copy-start(bf16[512,512]{0,1:T(8,128)(2,1)} %copy-done.13) | copy-start | bytes 1572868
  203.6 63.8 %copy-start.12 = (bf16[512,512]{0,1:T(8,128)(2,1)S(1)}, bf16[512,512]{0,1:T(8,128)(2,1)}, u32[]{:S(2)}) copy-start(bf16[512,512]{0,1:T(8,128)(2,1)} %copy-done.11) | copy-start | bytes 1572868
  203.6 64.6 %copy-start.10 = (bf16[512,512]{0,1:T(8,128)(2,1)S(1)}, bf16[512,512]{0,1:T(8,128)(2,1)}, u32[]{:S(2)}) copy-start(bf16[512,512]{0,1:T(8,128)(2,1)} %copy-done.9) | copy-start | bytes 1572868
  203.6 65.4 %copy-start.8 = (bf16[512,512]{0,1:T(8,128)(2,1)S(1)}, bf16[512,512]{0,1:T(8,128)(2,1)}, u32[]{:S(2)}) copy-start(bf16[512,512]{0,1:T(8,128)(2,1)} %copy-done.7) | copy-start | bytes 1572868
  203.6 66.3 %copy-start.6 = (bf16[512,512]{0,1:T(8,128)(2,1)S(1)}, bf16[512,512]{0,1:T(8,128)(2,1)}, u32[]{:S(2)}) copy-start(bf16[512,512]{0,1:T(8,128)(2,1)} %copy-done.5) | copy-start | bytes 1572868
  203.6 67.1 %copy-start.4 = (bf16[512,512]{0,1:T(8,128)(2,1)S(1)}, bf16[512,512]{0,1:T(8,128)(2,1)}, u32[]{:S(2)}) copy-start(bf16[512,512]{0,1:T(8,128)(2,1)} %copy-done.3) | copy-start | bytes 1572868
  203.7 68.0 %copy-start.2 = (bf16[512,512]{0,1:T(8,128)(2,1)S(1)}, bf16[512,512]{0,1:T(8,128)(2,1)}, u32[]{:S(2)}) copy-start(bf16[512,512]{0,1:T(8,128)(2,1)} %copy-done.1) | copy-start | bytes 1572868
  215.2 11.5 %collective-permute-start.13 = (bf16[512,512]{0,1:T(8,128)(2,1)}, bf16[512,512]{0,1:T(8,128)(2,1)S(1)}, u32[]{:S(2)}, u32[]{:S(2)}) collective-permute-start(bf16[512,512]{0,1:T(8,128)(2,1)} %collective-permute-done.12), channel_id=1, source_target_pairs={{0,1},{1,2},{2,3},{3,4},{4,5},{5,6},{6,7},{7,8},{8,9},{9,10},{10,1... | collective-permute-start | bytes 1572872 | tf_op jit(solution)/shard_map/ppermute | solution.py:30
  226.7 11.3 %collective-permute-start.14 = (bf16[512,512]{0,1:T(8,128)(2,1)S(1)}, bf16[512,512]{0,1:T(8,128)(2,1)S(1)}, u32[]{:S(2)}, u32[]{:S(2)}) collective-permute-start(bf16[512,512]{0,1:T(8,128)(2,1)S(1)} %collective-permute-done.13), channel_id=1, source_target_pairs={{0,1},{1,2},{2,3},{3,4},{4,5},{5,6},{6,7},{7,8},{8,9},{9,10},{10,1... | collective-permute-start | bytes 1572872 | tf_op jit(solution)/shard_map/ppermute | solution.py:30
  (7 other events, 5.7 us)
Sparse Core Ops, SparseCore 0:
  9.6 123.4 all-gather.1
